TPU v7x, 512 devices: a whole 4x4x16 slice. The times are simulated.
512 devices in a mesh: shard: 64 (over z, x), tensor: 4 (over y), section: 2 (over core).
Axes of the slice: x: 4, y: 4, z: 16, core: 2. Of those that a mesh axis runs over, the one named last changes fastest.
Arguments:
- query_key: float32 [2, 2, 1024, 1024], P('section', None, 'shard', 'tensor'), may hold values from -52 to 52, as said below
- query_key_gradient: float32 [2, 2, 1024, 1024], P('section', None, 'shard', 'tensor'), may hold values from -52 to 52
- query_key_first: float32 [2, 2, 1024, 1024], P('section', None, 'shard', 'tensor'), may hold values from -5.2 to 5.2
- query_key_second: float32 [2, 2, 1024, 1024], P('section', None, 'shard', 'tensor'), may hold values from 0.01 to 1
- value_gate: float32 [2, 2, 1024, 2048], P('section', None, 'shard', 'tensor'), may hold values from -52 to 52
- value_gate_gradient: float32 [2, 2, 1024, 2048], P('section', None, 'shard', 'tensor'), may hold values from -52 to 52
- value_gate_first: float32 [2, 2, 1024, 2048], P('section', None, 'shard', 'tensor'), may hold values from -5.2 to 5.2
- value_gate_second: float32 [2, 2, 1024, 2048], P('section', None, 'shard', 'tensor'), may hold values from 0.01 to 1
- output_weight: float32 [2, 2048, 1024], P('section', 'tensor', 'shard'), may hold values from -52 to 52
- output_gradient: float32 [2, 2048, 1024], P('section', 'tensor', 'shard'), may hold values from -52 to 52
- output_first: float32 [2, 2048, 1024], P('section', 'tensor', 'shard'), may hold values from -5.2 to 5.2
- output_second: float32 [2, 2048, 1024], P('section', 'tensor', 'shard'), may hold values from 0.01 to 1
- norm_gain: float32 [2, 1024], P('section', 'shard'), may hold values from -52 to 52
- gain_gradient: float32 [2, 1024], P('section', 'shard'), may hold values from -52 to 52
- gain_first: float32 [2, 1024], P('section', 'shard'), may hold values from -5.2 to 5.2
- gain_second: float32 [2, 1024], P('section', 'shard'), may hold values from 0.01 to 1
Outputs:
- new_query_key: float32 [2, 2, 1024, 1024], P('section', None, 'shard', 'tensor')
- new_query_key_first: float32 [2, 2, 1024, 1024], P('section', None, 'shard', 'tensor')
- new_query_key_second: float32 [2, 2, 1024, 1024], P('section', None, 'shard', 'tensor')
- new_value_gate: float32 [2, 2, 1024, 2048], P('section', None, 'shard', 'tensor')
- new_value_gate_first: float32 [2, 2, 1024, 2048], P('section', None, 'shard', 'tensor')
- new_value_gate_second: float32 [2, 2, 1024, 2048], P('section', None, 'shard', 'tensor')
- new_output: float32 [2, 2048, 1024], P('section', 'tensor', 'shard')
- new_output_first: float32 [2, 2048, 1024], P('section', 'tensor', 'shard')
- new_output_second: float32 [2, 2048, 1024], P('section', 'tensor', 'shard')
- new_gain: float32 [2, 1024], P('section', 'shard')
- new_gain_first: float32 [2, 1024], P('section', 'shard')
- new_gain_second: float32 [2, 1024], P('section', 'shard')
- copy_query_key: bfloat16 [2, 2, 1024, 1024], P('section', None, None, 'tensor')
- copy_value_gate: bfloat16 [2, 2, 1024, 2048], P('section', None, None, 'tensor')
- copy_output: bfloat16 [2, 2048, 1024], P('section', 'tensor')
- copy_gain: bfloat16 [2, 1024], P('section')
Inputs may be any that keep to these rules, and one draw needn't show every extreme that they name: `query_key`: projection weights, gradients and first moments are real-valued with entries of differing scale.
All inputs are finite; a program needn't handle non-finite values.
Results may differ from a plain program's by a relative error of at most 0.001.
Values may be sent and summed in bfloat16 or wider, within the bound.
A program may use at most 64 MiB of HBM per device.

v0:
```python
import jax
import jax.numpy as jnp
from jax import lax
from jax.sharding import PartitionSpec as P

STEP = 10
beta_one = 0.9
beta_two = 0.999
epsilon = 1e-06
learn_rate = 0.2


def local_terms(weight, gradient, first, second, decay, matrix_dims):
    first_new = beta_one * first + (1.0 - beta_one) * gradient
    second_new = beta_two * second + (1.0 - beta_two) * gradient * gradient
    update = (
        first_new
        / (1.0 - beta_one**STEP)
        / (jnp.sqrt(second_new / (1.0 - beta_two**STEP)) + epsilon)
        + decay * weight
    )
    norm_axes = tuple(range(weight.ndim - matrix_dims, weight.ndim))
    weight_sq = jnp.sum(weight * weight, axis=norm_axes)
    update_sq = jnp.sum(update * update, axis=norm_axes)
    return (first_new, second_new, update, weight_sq, update_sq)


def apply_trust(weight, update, weight_sq, update_sq, matrix_dims):
    trust = jnp.sqrt(weight_sq) / (jnp.sqrt(update_sq) + epsilon)
    trust = trust.reshape(trust.shape + (1,) * matrix_dims)
    return weight - learn_rate * trust * update


def on_device(
    query_key,
    query_key_gradient,
    query_key_first,
    query_key_second,
    value_gate,
    value_gate_gradient,
    value_gate_first,
    value_gate_second,
    output_weight,
    output_gradient,
    output_first,
    output_second,
    norm_gain,
    gain_gradient,
    gain_first,
    gain_second,
):
    qk_terms = local_terms(
        query_key, query_key_gradient, query_key_first, query_key_second, 0.01, 2
    )
    vg_terms = local_terms(
        value_gate, value_gate_gradient, value_gate_first, value_gate_second, 0.01, 2
    )
    output_terms = local_terms(output_weight, output_gradient, output_first, output_second, 0.01, 2)
    gain_terms = local_terms(norm_gain, gain_gradient, gain_first, gain_second, 0.0, 1)
    qk_sq = lax.psum((qk_terms[3], qk_terms[4]), ("shard", "tensor"))
    vg_sq = lax.psum((vg_terms[3], vg_terms[4]), ("shard", "tensor"))
    output_sq = lax.psum((output_terms[3], output_terms[4]), ("shard", "tensor"))
    gain_sq = lax.psum((gain_terms[3], gain_terms[4]), "shard")
    new_qk = apply_trust(query_key, qk_terms[2], qk_sq[0], qk_sq[1], 2)
    new_vg = apply_trust(value_gate, vg_terms[2], vg_sq[0], vg_sq[1], 2)
    new_output = apply_trust(output_weight, output_terms[2], output_sq[0], output_sq[1], 2)
    new_gain = apply_trust(norm_gain, gain_terms[2], gain_sq[0], gain_sq[1], 1)
    qk_half = new_qk.astype(jnp.bfloat16)
    vg_half = new_vg.astype(jnp.bfloat16)
    output_half = new_output.astype(jnp.bfloat16)
    gain_half = new_gain.astype(jnp.bfloat16)
    copy_qk = lax.all_gather(qk_half, "shard", axis=2, tiled=True)
    copy_vg = lax.all_gather(vg_half, "shard", axis=2, tiled=True)
    copy_output = lax.all_gather(output_half, "shard", axis=2, tiled=True)
    copy_gain = lax.all_gather(gain_half, "shard", axis=1, tiled=True)
    return (
        new_qk,
        qk_terms[0],
        qk_terms[1],
        new_vg,
        vg_terms[0],
        vg_terms[1],
        new_output,
        output_terms[0],
        output_terms[1],
        new_gain,
        gain_terms[0],
        gain_terms[1],
        copy_qk,
        copy_vg,
        copy_output,
        copy_gain,
    )


def solution(mesh):
    placed = (
        P("section", None, "shard", "tensor"),
        P("section", None, "shard", "tensor"),
        P("section", None, "shard", "tensor"),
        P("section", None, "shard", "tensor"),
        P("section", None, "shard", "tensor"),
        P("section", None, "shard", "tensor"),
        P("section", None, "shard", "tensor"),
        P("section", None, "shard", "tensor"),
        P("section", "tensor", "shard"),
        P("section", "tensor", "shard"),
        P("section", "tensor", "shard"),
        P("section", "tensor", "shard"),
        P("section", "shard"),
        P("section", "shard"),
        P("section", "shard"),
        P("section", "shard"),
    )
    return jax.shard_map(
        on_device,
        mesh=mesh,
        in_specs=placed,
        out_specs=(
            P("section", None, "shard", "tensor"),
            P("section", None, "shard", "tensor"),
            P("section", None, "shard", "tensor"),
            P("section", None, "shard", "tensor"),
            P("section", None, "shard", "tensor"),
            P("section", None, "shard", "tensor"),
            P("section", "tensor", "shard"),
            P("section", "tensor", "shard"),
            P("section", "tensor", "shard"),
            P("section", "shard"),
            P("section", "shard"),
            P("section", "shard"),
            P("section", None, None, "tensor"),
            P("section", None, None, "tensor"),
            P("section", "tensor", None),
            P("section", None),
        ),
        check_vma=False,
    )
```

profile of v0, /device:TPU:8, one launch (start us, length us, event | category | flops | bytes accessed | tf_op | source)
XLA Modules:
  0.0 1120.5 jit_solution(3101346954064736465)
XLA Ops:
  7.2 0.0 all-gather.4.cloned.1.call-start
  7.2 1.1 multiply_reduce_fusion.1
  8.3 1.0 multiply_reduce_fusion.5
  9.3 1.5 multiply_reduce_fusion.2
  10.8 691.5 %all-reduce.1 = (f32[1,2]{1,0:T(1,128)S(1)}, f32[1,2]{1,0:T(1,128)S(1)}, f32[1,2]{1,0:T(1,128)S(1)}, f32[1,2]{1,0:T(1,128)S(1)}, f32[1]{0:T(128)}, /*index=5*/f32[1]{0:T(128)}) all-reduce(f32[1,2]{1,0:T(1,128)S(1)} %bitcast.20, f32[1,2]{1,0:T(1,128)S(1)} %bitcast.19, ...), channel_id=1, replica_groups=mesh['shard'=64,'tensor'=4,'section'=2] {'shard','tensor'}, use_global_device_ids=true, to_apply=%region_3.0 | all-reduce | flops 10 | bytes 80 | tf_op jit(solution)/shard_map/psum | solution.py:60
  702.3 1.5 fusion.6
  703.8 0.0 all-gather.4.cloned.1.call-update
  703.8 0.0 all-gather.8.cloned.1.call-start
  705.2 1.4 fusion.4
  706.6 0.0 all-gather.8.cloned.1.call-update
  706.7 0.0 all-gather.6.cloned.1.call-start
  706.7 1.6 fusion.5
  708.3 0.0 all-gather.6.cloned.1.call-update
  708.3 1.8 multiply_reduce_fusion.6
  710.1 138.7 %all-reduce.2 = (f32[1]{0:T(128)}, f32[1]{0:T(128)}) all-reduce(f32[1]{0:T(128)} %bitcast.9, f32[1]{0:T(128)} %bitcast.10), channel_id=1, replica_groups=mesh['shard'=64,'tensor'=4,'section'=2] {'shard'}, use_global_device_ids=true, to_apply=%region_13.0 | all-reduce | flops 2 | bytes 16 | tf_op jit(solution)/shard_map/psum | solution.py:63
  850.3 1.3 dynamic-slice
  852.2 1.2 convert_bitcast_fusion
  853.4 0.2 dynamic-update-slice
  853.5 140.4 %all-reduce = bf16[1024]{0:T(1024)(128)(2,1)S(1)} all-reduce(bf16[1024]{0:T(1024)(128)(2,1)S(1)} %dynamic-update-slice), channel_id=1, replica_groups=mesh['shard'=64,'tensor'=4,'section'=2] {'shard'}, use_global_device_ids=true, to_apply=%add | all-reduce | flops 1024 | bytes 4096
  993.9 0.6 reshape.78
  994.5 2.4 copy.33
  996.9 113.8 %all-gather.6.cloned.1.call-done = bf16[1,2,1024,512]{3,2,1,0:T(8,128)(2,1)} async-done(((bf16[1,2,16,512]{3,2,1,0:T(8,128)(2,1)}), bf16[1,2,1024,512]{3,2,1,0:T(8,128)(2,1)}) %all-gather.6.cloned.1.call-update) | async-done | bytes 2097168 | tf_op jit(solution)/shard_map/all_gather | solution.py:73
  1110.7 0.0 copy-done.1
  1110.7 1.0 copy.37
  1111.6 0.0 copy-done.2
  1111.7 0.0 copy-done.3
  1111.7 0.0 copy-done.4
  1111.7 0.0 copy-done.5
  1111.7 0.0 copy-done.6
  1111.7 0.0 copy-done.7
  1111.7 1.0 copy-done
  1112.6 1.3 copy.38
  (12 shorter events, 0.0 us)
Async XLA Ops:
  7.2 987.3 %all-gather.4.cloned.1.call-start = ((), (), s32[]{:S(2)}) async-start(), calls=%async_computation | async-start | bytes 1064960 | tf_op jit(solution)/shard_map/all_gather | solution.py:72
  8.3 1103.3 %copy-start.2 = (f32[1,2,16,512]{3,2,1,0:T(8,128)}, f32[1,2,16,512]{3,2,1,0:T(8,128)S(1)}, u32[]{:S(2)}) copy-start(f32[1,2,16,512]{3,2,1,0:T(8,128)S(1)} %get-tuple-element.87) | copy-start | bytes 196612
  8.3 1103.3 %copy-start.3 = (f32[1,2,16,512]{3,2,1,0:T(8,128)}, f32[1,2,16,512]{3,2,1,0:T(8,128)S(1)}, u32[]{:S(2)}) copy-start(f32[1,2,16,512]{3,2,1,0:T(8,128)S(1)} %get-tuple-element.88) | copy-start | bytes 196612
  9.3 1102.3 %copy-start.4 = (f32[1,2,16,256]{3,2,1,0:T(8,128)}, f32[1,2,16,256]{3,2,1,0:T(8,128)S(1)}, u32[]{:S(2)}) copy-start(f32[1,2,16,256]{3,2,1,0:T(8,128)S(1)} %get-tuple-element.84) | copy-start | bytes 98308
  9.3 1102.3 %copy-start.5 = (f32[1,2,16,256]{3,2,1,0:T(8,128)}, f32[1,2,16,256]{3,2,1,0:T(8,128)S(1)}, u32[]{:S(2)}) copy-start(f32[1,2,16,256]{3,2,1,0:T(8,128)S(1)} %get-tuple-element.85) | copy-start | bytes 98308
  10.8 1100.9 %copy-start.6 = (f32[1,512,16]{1,2,0:T(8,128)}, f32[1,512,16]{1,2,0:T(8,128)S(1)}, u32[]{:S(2)}) copy-start(f32[1,512,16]{1,2,0:T(8,128)S(1)} %get-tuple-element.90) | copy-start | bytes 98308
  10.8 1100.9 %copy-start.7 = (f32[1,512,16]{1,2,0:T(8,128)}, f32[1,512,16]{1,2,0:T(8,128)S(1)}, u32[]{:S(2)}) copy-start(f32[1,512,16]{1,2,0:T(8,128)S(1)} %get-tuple-element.91) | copy-start | bytes 98308
  703.8 290.7 %all-gather.8.cloned.1.call-start = ((), (), s32[]{:S(2)}) async-start(), calls=%async_computation.2 | async-start | bytes 1064960 | tf_op jit(solution)/shard_map/all_gather | solution.py:74
  706.7 404.0 %all-gather.6.cloned.1.call-start = ((), (), s32[]{:S(2)}) async-start(), calls=%async_computation.1 | async-start | bytes 2129920 | tf_op jit(solution)/shard_map/all_gather | solution.py:73
  994.5 116.2 %copy-start.1 = (bf16[1,2,1024,256]{3,2,1,0:T(8,128)(2,1)S(1)}, bf16[1,2,1024,256]{3,2,1,0:T(8,128)(2,1)}, u32[]{:S(2)}) copy-start(bf16[1,2,1024,256]{3,2,1,0:T(8,128)(2,1)} %all-gather.4.cloned.1.call-done) | copy-start | bytes 3145732
  1110.7 2.0 copy-start
Sparse Core Ops, SparseCore 0:
  703.9 128.1 all-gather.3
  835.6 134.3 all-gather.7
  973.5 137.0 all-gather.5
where the time goes:
time: 1120 us
  blocking collectives  971 us (87%)
  waiting for transfers between devices  114 us (10%)
  between operations  17.3 us (2%)
    psum x1, blocking collectives, on_device(): qk_sq = lax.psum((qk_terms[3], qk_terms[4]), ('shard', 'tensor'))  691 us
    unnamed x1, blocking collectives  140 us
    psum x1, blocking collectives, on_device(): gain_sq = lax.psum((gain_terms[3], gain_terms[4]), 'shard')  139 us
    all_gather x1, waiting for transfers between devices, on_device(): copy_vg = lax.all_gather(vg_half, 'shard', axis=2, tiled=True)  114 us
  transfers between devices with their start and end apart: 3, of which 1 were waited for; matrix products, arithmetic and copies ran while one was open for 1% of the time, Pallas kernels for 0%

commit v1 on v0

--- a/solution.py
+++ b/solution.py
@@ -57,7 +57,7 @@
     )
     output_terms = local_terms(output_weight, output_gradient, output_first, output_second, 0.01, 2)
     gain_terms = local_terms(norm_gain, gain_gradient, gain_first, gain_second, 0.0, 1)
-    qk_sq = lax.psum((qk_terms[3], qk_terms[4]), ("shard", "tensor"))
+    qk_sq = lax.psum(lax.psum((qk_terms[3], qk_terms[4]), "shard"), "tensor")
     vg_sq = lax.psum((vg_terms[3], vg_terms[4]), ("shard", "tensor"))
     output_sq = lax.psum((output_terms[3], output_terms[4]), ("shard", "tensor"))
     gain_sq = lax.psum((gain_terms[3], gain_terms[4]), "shard")

time: 1120 us -> 1140 us (1.018)
  blocking collectives: 971 us -> 983 us
    psum x2 -> x3, blocking collectives: 830 us -> 845 us  [the longest x1 686 us: on_device(): vg_sq = lax.psum((vg_terms[3], vg_terms[4]), ('shard', 'tensor'))]
where the time goes in v1:
time: 1140 us
  blocking collectives  983 us (86%)
  waiting for transfers between devices  123 us (11%)
  between operations  17.3 us (2%)
    psum x1, blocking collectives, on_device(): vg_sq = lax.psum((vg_terms[3], vg_terms[4]), ('shard', 'tensor'))  686 us
    psum x2, blocking collectives, on_device(): qk_sq = lax.psum(lax.psum((qk_terms[3], qk_terms[4]), 'shard'), 'tensor')  159 us
    unnamed x1, blocking collectives  138 us
    all_gather x1, waiting for transfers between devices, on_device(): copy_vg = lax.all_gather(vg_half, 'shard', axis=2, tiled=True)  123 us
  transfers between devices with their start and end apart: 3, of which 1 were waited for; matrix products, arithmetic and copies ran while one was open for 1% of the time, Pallas kernels for 0%

profile of v1, /device:TPU:8, one launch (start us, length us, event | category | flops | bytes accessed | tf_op | source)
XLA Modules:
  0.0 1142.6 jit_solution(8854837798130464971)
XLA Ops:
  7.2 0.0 all-gather.4.cloned.1.call-start
  7.2 1.8 multiply_reduce_fusion.6
  9.1 0.9 multiply_reduce_fusion.5
  10.0 150.3 %all-reduce.2 = (f32[1,2]{1,0:T(1,128)S(1)}, f32[1,2]{1,0:T(1,128)S(1)}, f32[1]{0:T(128)}, f32[1]{0:T(128)}) all-reduce(f32[1,2]{1,0:T(1,128)S(1)} %bitcast.18, f32[1,2]{1,0:T(1,128)S(1)} %bitcast.17, f32[1]{0:T(128)} %bitcast.9, f32[1]{0:T(128)} %bitcast.10), channel_id=1, replica_groups=mesh['shard'=64,'tensor'=4,'section'=2] {'shard'}, use_global_device_ids=true, to_apply=%region_4.0 | all-reduce | flops 6 | bytes 48 | tf_op jit(solution)/shard_map/psum | solution.py:60
  160.3 8.7 all-reduce.3
  169.0 1.5 fusion.6
  170.4 0.0 all-gather.4.cloned.1.call-update
  170.4 0.0 all-gather.8.cloned.1.call-start
  170.5 1.5 multiply_reduce_fusion.2
  172.0 1.1 multiply_reduce_fusion.1
  173.1 686.1 %all-reduce.1 = (f32[1,2]{1,0:T(1,128)S(1)}, f32[1,2]{1,0:T(1,128)S(1)}, f32[1]{0:T(128)}, f32[1]{0:T(128)}) all-reduce(f32[1,2]{1,0:T(1,128)S(1)} %bitcast.20, f32[1,2]{1,0:T(1,128)S(1)} %bitcast.19, f32[1]{0:T(128)} %bitcast.6, f32[1]{0:T(128)} %bitcast.7), channel_id=1, replica_groups=mesh['shard'=64,'tensor'=4,'section'=2] {'shard','tensor'}, use_global_device_ids=true, to_apply=%region_9.0 | all-reduce | flops 6 | bytes 48 | tf_op jit(solution)/shard_map/psum | solution.py:61
  860.7 1.4 fusion.4
  862.1 0.0 all-gather.8.cloned.1.call-update
  862.1 0.0 all-gather.6.cloned.1.call-start
  862.1 1.6 fusion.5
  863.7 0.0 all-gather.6.cloned.1.call-update
  865.1 1.3 dynamic-slice
  867.1 1.2 convert_bitcast_fusion
  868.2 0.2 dynamic-update-slice
  868.4 138.3 %all-reduce = bf16[1024]{0:T(1024)(128)(2,1)S(1)} all-reduce(bf16[1024]{0:T(1024)(128)(2,1)S(1)} %dynamic-update-slice), channel_id=1, replica_groups=mesh['shard'=64,'tensor'=4,'section'=2] {'shard'}, use_global_device_ids=true, to_apply=%add | all-reduce | flops 1024 | bytes 4096
  1006.7 0.6 reshape.78
  1007.3 2.4 copy.33
  1009.6 123.1 %all-gather.6.cloned.1.call-done = bf16[1,2,1024,512]{3,2,1,0:T(8,128)(2,1)} async-done(((bf16[1,2,16,512]{3,2,1,0:T(8,128)(2,1)}), bf16[1,2,1024,512]{3,2,1,0:T(8,128)(2,1)}) %all-gather.6.cloned.1.call-update) | async-done | bytes 2097168 | tf_op jit(solution)/shard_map/all_gather | solution.py:73
  1132.7 0.0 copy-done.1
  1132.7 1.0 copy.37
  1133.7 0.0 copy-done.4
  1133.7 0.0 copy-done.5
  1133.7 0.0 copy-done.6
  1133.7 0.0 copy-done.7
  1133.7 0.0 copy-done.2
  1133.7 1.0 copy-done
  1134.7 1.3 copy.38
  (14 shorter events, 0.0 us)
Async XLA Ops:
  7.2 1000.1 %all-gather.4.cloned.1.call-start = ((), (), s32[]{:S(2)}) async-start(), calls=%async_computation | async-start | bytes 1064960 | tf_op jit(solution)/shard_map/all_gather | solution.py:72
  10.0 1123.7 %copy-start.4 = (f32[1,2,16,256]{3,2,1,0:T(8,128)}, f32[1,2,16,256]{3,2,1,0:T(8,128)S(1)}, u32[]{:S(2)}) copy-start(f32[1,2,16,256]{3,2,1,0:T(8,128)S(1)} %get-tuple-element.84) | copy-start | bytes 98308
  10.0 1123.7 %copy-start.5 = (f32[1,2,16,256]{3,2,1,0:T(8,128)}, f32[1,2,16,256]{3,2,1,0:T(8,128)S(1)}, u32[]{:S(2)}) copy-start(f32[1,2,16,256]{3,2,1,0:T(8,128)S(1)} %get-tuple-element.85) | copy-start | bytes 98308
  170.4 836.8 %all-gather.8.cloned.1.call-start = ((), (), s32[]{:S(2)}) async-start(), calls=%async_computation.2 | async-start | bytes 1064960 | tf_op jit(solution)/shard_map/all_gather | solution.py:74
  172.0 961.8 %copy-start.6 = (f32[1,512,16]{1,2,0:T(8,128)}, f32[1,512,16]{1,2,0:T(8,128)S(1)}, u32[]{:S(2)}) copy-start(f32[1,512,16]{1,2,0:T(8,128)S(1)} %get-tuple-element.90) | copy-start | bytes 98308
  172.0 961.8 %copy-start.7 = (f32[1,512,16]{1,2,0:T(8,128)}, f32[1,512,16]{1,2,0:T(8,128)S(1)}, u32[]{:S(2)}) copy-start(f32[1,512,16]{1,2,0:T(8,128)S(1)} %get-tuple-element.91) | copy-start | bytes 98308
  173.1 960.6 %copy-start.2 = (f32[1,2,16,512]{3,2,1,0:T(8,128)}, f32[1,2,16,512]{3,2,1,0:T(8,128)S(1)}, u32[]{:S(2)}) copy-start(f32[1,2,16,512]{3,2,1,0:T(8,128)S(1)} %get-tuple-element.87) | copy-start | bytes 196612
  173.1 960.7 %copy-start.3 = (f32[1,2,16,512]{3,2,1,0:T(8,128)}, f32[1,2,16,512]{3,2,1,0:T(8,128)S(1)}, u32[]{:S(2)}) copy-start(f32[1,2,16,512]{3,2,1,0:T(8,128)S(1)} %get-tuple-element.88) | copy-start | bytes 196612
  862.1 270.7 %all-gather.6.cloned.1.call-start = ((), (), s32[]{:S(2)}) async-start(), calls=%async_computation.1 | async-start | bytes 2129920 | tf_op jit(solution)/shard_map/all_gather | solution.py:73
  1007.3 125.4 %copy-start.1 = (bf16[1,2,1024,256]{3,2,1,0:T(8,128)(2,1)S(1)}, bf16[1,2,1024,256]{3,2,1,0:T(8,128)(2,1)}, u32[]{:S(2)}) copy-start(bf16[1,2,1024,256]{3,2,1,0:T(8,128)(2,1)} %all-gather.4.cloned.1.call-done) | copy-start | bytes 3145732
  1132.7 2.0 copy-start
Sparse Core Ops, SparseCore 0:
  170.6 123.8 all-gather.3
  862.2 129.8 all-gather.7
  995.6 137.0 all-gather.5
